TPU v7x, 32 devices: a whole 2x2x4 slice. The times are simulated.
32 devices in a mesh: seq: 16 (over z, x, core), tp: 2 (over y).
Axes of the slice: x: 2, y: 2, z: 4, core: 2. Of those that a mesh axis runs over, the one named last changes fastest.
Arguments:
- normed_input: bfloat16 [2048, 4096], P(('seq', 'tp')), may hold values from -6 to 6
- output_gradient: bfloat16 [2048, 14336], P('seq', 'tp'), may hold values from -0.75 to 0.75
- adapter_down: bfloat16 [64, 16, 4096], P('seq', None, 'tp'), may hold values from -0.09375 to 0.09375
- adapter_up: bfloat16 [64, 16, 14336], P('seq', None, 'tp'), may hold values from -1.5 to 1.5
- adapter_of_block: int32 [16], P('seq'), may hold values from 0 to 63
- live_per_block: int32 [16], P('seq'), may hold values from 32 to 128, as said below
- adapter_home_row: int32 [64], replicated, may hold values from 0 to 63, each once
Outputs:
- adapter_output: bfloat16 [2048, 14336], P('seq', 'tp')
- input_gradient: bfloat16 [2048, 4096], P(('seq', 'tp'))
- down_gradient: float32 [64, 16, 4096], P('seq', None, 'tp')
- up_gradient: float32 [64, 16, 14336], P('seq', None, 'tp')
Inputs may be any that keep to these rules, and one draw needn't show every extreme that they name: `live_per_block`: every eighth block, counting from block 0, is full. `adapter_home_row`: each row appears once.
All inputs are finite; a program needn't handle non-finite values.
Results may differ from a plain program's by a relative error of at most 0.0051.
Values may be sent and summed in bfloat16 or wider, within the bound.
A program may use at most 128 MiB of HBM per device.

v0:
```python
import functools

import jax
import jax.numpy as jnp
from jax import lax
from jax.experimental import pallas as pl
from jax.experimental.pallas import tpu as pltpu
from jax.sharding import PartitionSpec as P

adapter_scale = 2.0
GROUP = 4
MESH = pl.DeviceIdType.MESH
VMEM = pltpu.VMEM


def pieces(width, most):
    tiles = width // 128
    count = max(k for k in range(1, most + 1) if tiles % k == 0)
    step = width // count
    return [(i * step, step) for i in range(count)]


def greet(n, tp, me, mine):
    barrier = pltpu.get_barrier_semaphore()

    def seq_signal(d, carry):
        pl.semaphore_signal(barrier, inc=1, device_id=(lax.rem(me + d, n), mine), device_id_type=MESH)
        return carry

    lax.fori_loop(1, n, seq_signal, 0)
    for d in range(1, tp):
        pl.semaphore_signal(barrier, inc=1, device_id=(me, lax.rem(mine + d, tp)), device_id_type=MESH)
    pl.semaphore_wait(barrier, n - 1 + tp - 1)


def step_kernel(
    n, tp, a_ref, b_ref, x_ref, g_ref, id_ref, live_ref,
    down_out, b_out, grad_a, grad_b, x_out,
    fa, fb, sa, sb, za, zb, ga, gb, pick_a, xt, g, ids, part, gx,
    raw_send, raw_recv, z_send, z_recv, grad_send, grad_recv, far_send, far_recv,
    id_send, id_recv, x_send, x_recv, part_send, part_recv, gx_send, gx_recv, local_sem,
):
    me, mine = lax.axis_index("seq"), lax.axis_index("tp")
    planes = n // GROUP
    plane, spot = me // GROUP, lax.rem(me, GROUP)
    near = me + 1 - 2 * lax.rem(spot, 2)
    far = me + 2 - 4 * (spot // 2)
    far_spot = spot + 2 - 4 * (spot // 2)
    rows = a_ref.shape[0]
    rank = pick_a.shape[0]
    total = fa.shape[0]
    width = xt.shape[2]
    tokens = g.shape[0]
    slots = rows // rank
    column = planes * rank
    f32, low = jnp.float32, jnp.bfloat16

    def remote(src, dst, send, recv, seq_at, tp_at):
        return pltpu.make_async_remote_copy(
            src_ref=src, dst_ref=dst, send_sem=send, recv_sem=recv,
            device_id=(seq_at, tp_at), device_id_type=MESH,
        )

    def columns(index):
        return pl.ds(pl.multiple_of(index * width, width), width)

    own = pl.ds(pl.multiple_of(spot * rows, rows), rows)
    other = pl.ds(pl.multiple_of(far_spot * rows, rows), rows)
    local = [
        pltpu.make_async_copy(a_ref, fa.at[own, :], local_sem.at[0]),
        pltpu.make_async_copy(b_ref, fb.at[own, :], local_sem.at[1]),
        pltpu.make_async_copy(x_ref.at[:, columns(mine)], xt.at[mine], local_sem.at[2]),
        pltpu.make_async_copy(g_ref, g, local_sem.at[3]),
    ]
    for copy in local:
        copy.start()
    greet(n, tp, me, mine)

    def id_copy(d):
        return remote(id_ref, ids.at[me], id_send.at[d], id_recv.at[d], lax.rem(me + d, n), mine)

    lax.fori_loop(1, n, lambda d, c: (id_copy(d).start(), c)[1], 0)

    a_cuts, b_cuts = pieces(a_ref.shape[1], 2), pieces(b_ref.shape[1], 7)
    cuts = [(a_ref, fa, sa, za, *cut) for cut in a_cuts] + [(b_ref, fb, sb, zb, *cut) for cut in b_cuts]
    to_far, to_near, forward = [], [], []
    for j, (src, full, _, _, start, size) in enumerate(cuts):
        cols = pl.ds(start, size)
        to_far.append(remote(src.at[:, cols], full.at[own, cols], raw_send.at[0, j], raw_recv.at[0, j], far, mine))
        to_near.append(remote(src.at[:, cols], full.at[own, cols], raw_send.at[1, j], raw_recv.at[1, j], near, mine))
        forward.append(remote(full.at[other, cols], full.at[other, cols], raw_send.at[2, j], raw_recv.at[2, j], near, mine))
        to_far[j].start()
        to_near[j].start()
    x_copies = []
    for d in range(1, tp):
        peer = lax.rem(mine + d, tp)
        x_copies.append(remote(x_ref.at[:, columns(peer)], xt.at[mine], x_send.at[d], x_recv.at[d], me, peer))
        x_copies[-1].start()
    ids[me] = id_ref[...]
    for copy in local:
        copy.wait()
    lax.fori_loop(1, n, lambda d, c: (id_copy(d).wait(), c)[1], 0)

    base = plane * (total // rank)
    row_at = lax.broadcasted_iota(jnp.int32, (rank, total), 0)
    col_at = lax.broadcasted_iota(jnp.int32, (rank, total), 1)
    picks = []
    for p in range(planes):
        wanted = jnp.broadcast_to(ids[p * GROUP + spot, 0:1, 0:1], (rank, total)) - base
        picks.append((col_at == wanted * rank + row_at).astype(f32))
    pick = jnp.concatenate(picks, axis=0).astype(low)
    place_row = lax.broadcasted_iota(jnp.int32, (rows, n * rank), 0)
    place_col = lax.broadcasted_iota(jnp.int32, (rows, n * rank), 1)
    target = jnp.full((rows, n * rank), -1, jnp.int32)
    for p in range(planes):
        for q in range(GROUP):
            first = (q * planes + p) * rank
            home = jnp.broadcast_to(ids[p * GROUP + q, 1:2, 0:1], (rows, n * rank))
            at = (home - me * slots) * rank + place_col - first
            target = jnp.where((place_col >= first) & (place_col < first + rank), at, target)
    place = (target == place_row).astype(f32).astype(low)

    z_copies = []

    def choose(j):
        _, full, chosen, landed, start, size = cuts[j]
        cols = pl.ds(start, size)
        to_far[j].wait_recv()
        forward[j].start()
        to_near[j].wait_recv()
        forward[j].wait_recv()
        got = jnp.dot(pick, full[:, cols], preferred_element_type=f32).astype(low)
        chosen[:, :, cols] = got.reshape(planes, rank, size)
        for d in range(1, planes):
            to = lax.rem(plane + d, planes)
            copy = remote(
                chosen.at[to, :, cols], landed.at[d, :, cols],
                z_send.at[d, j], z_recv.at[d, j], to * GROUP + spot, mine,
            )
            copy.start()
            z_copies.append(copy)

    def settle(j, out):
        _, _, chosen, landed, start, size = cuts[j]
        cols = pl.ds(start, size)
        value = chosen[plane, :, cols].astype(f32)
        for d in range(1, planes):
            z_copies[j * (planes - 1) + d - 1].wait_recv()
            value += landed[d, :, cols].astype(f32)
        out[:, cols] = value.astype(low)

    def outer(left, right):
        return lax.dot_general(left, right, (((1,), (1,)), ((), ())), preferred_element_type=f32)

    part_copies = []

    def share(which, value):
        part[which, 0] = value
        for d in range(1, tp):
            copy = remote(
                part.at[which, 0], part.at[which, d], part_send.at[which, d], part_recv.at[which, d],
                me, lax.rem(mine + d, tp),
            )
            copy.start()
            part_copies.append(copy)

    def collect(which):
        value = part[which, 0]
        for d in range(1, tp):
            part_copies[which * (tp - 1) + d - 1].wait_recv()
            value = value + part[which, d]
        return value * live_ref[0:1, :]

    grads = [(gb, grad_b, *cut) for cut in b_cuts] + [(ga, grad_a, *cut) for cut in a_cuts]
    slot = pl.ds(pl.multiple_of(spot * column + plane * rank, rank), rank)
    mine_all = pl.ds(pl.multiple_of(spot * column, column), column)
    other_all = pl.ds(pl.multiple_of(far_spot * column, column), column)
    count = len(grads)
    spread_copies = [[] for _ in range(count)]
    far_copies, near_copies, pass_copies = [], [], []

    def spread(j):
        full, _, start, size = grads[j]
        cols = pl.ds(start, size)
        for d in range(1, planes):
            copy = remote(
                full.at[slot, cols], full.at[slot, cols], grad_send.at[d, j], grad_recv.at[d, j],
                lax.rem(plane + d, planes) * GROUP + spot, mine,
            )
            copy.start()
            spread_copies[j].append(copy)

    def cross(j):
        full, _, start, size = grads[j]
        cols = pl.ds(start, size)
        for copy in spread_copies[j]:
            copy.wait_recv()
        far_copies.append(remote(full.at[mine_all, cols], full.at[mine_all, cols], far_send.at[0, j], far_recv.at[0, j], far, mine))
        near_copies.append(remote(full.at[mine_all, cols], full.at[mine_all, cols], far_send.at[1, j], far_recv.at[1, j], near, mine))
        pass_copies.append(remote(full.at[other_all, cols], full.at[other_all, cols], far_send.at[2, j], far_recv.at[2, j], near, mine))
        far_copies[j].start()
        near_copies[j].start()

    def pass_on(j):
        far_copies[j].wait_recv()
        pass_copies[j].start()

    def finish(j):
        full, out, start, size = grads[j]
        cols = pl.ds(start, size)
        near_copies[j].wait_recv()
        pass_copies[j].wait_recv()
        out[:, cols] = jnp.dot(place, full[:, cols], preferred_element_type=f32)

    na, nb = len(a_cuts), len(b_cuts)
    for j in range(na + 2):
        choose(j)
    for j in range(na):
        settle(j, pick_a)
    for copy in x_copies:
        copy.wait()
    x_all = xt[...].reshape(tokens, width)
    share(0, outer(pick_a[...], x_all))
    choose(na + 2)
    down = collect(0).astype(low)
    down_out[...] = down
    for start, size in b_cuts:
        cols = pl.ds(start, size)
        gb[slot, cols] = (adapter_scale * jnp.dot(down, g[:, cols], preferred_element_type=f32)).astype(low)
    sent = 0
    for j in range(na + 3, na + nb):
        spread(sent)
        sent += 1
        choose(j)
    crossed = 0
    early = min(2, sent)
    for j in range(early):
        cross(j)
    crossed = early
    spread(sent)
    sent += 1
    total_back = jnp.zeros((rank, tokens), f32)
    for j in range(nb):
        settle(na + j, b_out)
        cols = pl.ds(*b_cuts[j])
        total_back = total_back + outer(b_out[:, cols], g[:, cols])
    share(1, total_back)
    while sent < nb:
        spread(sent)
        sent += 1
    while crossed < min(nb, 4):
        cross(crossed)
        crossed += 1
    back_full = adapter_scale * collect(1)
    back = back_full.astype(low)
    ga[slot, :] = jnp.dot(back, x_all, preferred_element_type=f32).astype(low)
    for j in range(nb, count):
        spread(j)
    back_t = back_full.T.astype(low)
    gx[...] = jnp.dot(back_t, pick_a[...], preferred_element_type=f32).astype(low).reshape(gx.shape)
    gx_copies = []
    for d in range(1, tp):
        peer = lax.rem(mine + d, tp)
        gx_copies.append(remote(gx.at[peer], x_out.at[:, columns(mine)], gx_send.at[d], gx_recv.at[d], me, peer))
        gx_copies[-1].start()
    x_out[:, columns(mine)] = gx[mine]
    passed, done = 0, 0
    while done < count:
        if crossed < count:
            cross(crossed)
            crossed += 1
        if passed < count and passed < crossed - (1 if crossed < count else 0):
            pass_on(passed)
            passed += 1
        if crossed == count:
            while passed < count and passed - done < 2:
                pass_on(passed)
                passed += 1
            finish(done)
            done += 1
        elif done < passed - 1:
            finish(done)
            done += 1
    for copy in gx_copies:
        copy.wait()
    for copy in to_far + to_near + forward + z_copies + part_copies:
        copy.wait_send()
    for group in spread_copies + [far_copies, near_copies, pass_copies]:
        for copy in group:
            copy.wait_send()


def step(n, tp, a, b, x, g, ids, live):
    slots, rank, width = a.shape
    hidden = b.shape[2]
    rows = x.shape[0]
    tokens = g.shape[0]
    planes = n // GROUP
    cuts = len(pieces(width, 2)) + len(pieces(hidden, 7))
    total = GROUP * slots * rank
    low, f32 = jnp.bfloat16, jnp.float32
    dma = pltpu.SemaphoreType.DMA
    anywhere = pl.BlockSpec(memory_space=pl.ANY)
    inside = pl.BlockSpec(memory_space=VMEM)
    return pl.pallas_call(
        functools.partial(step_kernel, n, tp),
        out_shape=(
            jax.ShapeDtypeStruct((rank, tokens), low),
            jax.ShapeDtypeStruct((rank, hidden), low),
            jax.ShapeDtypeStruct((slots * rank, width), f32),
            jax.ShapeDtypeStruct((slots * rank, hidden), f32),
            jax.ShapeDtypeStruct((rows, tp * width), low),
        ),
        in_specs=[anywhere] * 4 + [inside] * 2,
        out_specs=(inside,) * 5,
        scratch_shapes=[
            VMEM((total, width), low), VMEM((total, hidden), low),
            VMEM((planes, rank, width), low), VMEM((planes, rank, hidden), low),
            VMEM((planes, rank, width), low), VMEM((planes, rank, hidden), low),
            VMEM((n * rank, width), low), VMEM((n * rank, hidden), low),
            VMEM((rank, width), low), VMEM((tp, rows, width), low), VMEM((tokens, hidden), low),
            VMEM((n, 8, 128), jnp.int32), VMEM((2, tp, rank, tokens), f32), VMEM((tp, rows, width), low),
            dma((3, cuts)), dma((3, cuts)), dma((planes, cuts)), dma((planes, cuts)),
            dma((planes, cuts)), dma((planes, cuts)), dma((3, cuts)), dma((3, cuts)),
            dma((n,)), dma((n,)), dma((tp,)), dma((tp,)), dma((2, tp)), dma((2, tp)),
            dma((tp,)), dma((tp,)), dma((4,)),
        ],
        compiler_params=pltpu.CompilerParams(
            collective_id=0, has_side_effects=True, vmem_limit_bytes=56 * 1024 * 1024
        ),
    )(a.reshape(slots * rank, width), b.reshape(slots * rank, hidden), x, g, ids, live)


def per_device(
    normed_input,
    output_gradient,
    adapter_down,
    adapter_up,
    adapter_of_block,
    live_per_block,
    adapter_home_row,
):
    n, tp = lax.axis_size("seq"), lax.axis_size("tp")
    slots, rank, width = adapter_down.shape
    hidden = adapter_up.shape[2]
    tokens = output_gradient.shape[0]
    adapters = adapter_home_row.shape[0]
    f32, low = jnp.float32, jnp.bfloat16
    adapter = adapter_of_block[0]
    home = jnp.sum(jnp.where(jnp.arange(adapters, dtype=jnp.int32) == adapter, adapter_home_row, 0))
    ids = jnp.where(jnp.arange(8, dtype=jnp.int32)[:, None] == 0, adapter, home)
    ids = jnp.broadcast_to(ids, (8, 128))
    live = (jnp.arange(tokens, dtype=jnp.int32) < live_per_block[0]).astype(f32)
    live = jnp.broadcast_to(live[None, :], (8, tokens))
    down, pick_b, grad_a, grad_b, gx = step(
        n, tp, adapter_down, adapter_up, normed_input, output_gradient, ids, live
    )
    out = (adapter_scale * jnp.einsum("rt,rf->tf", down, pick_b, preferred_element_type=f32)).astype(low)
    return (out, gx, grad_a.reshape(slots, rank, width), grad_b.reshape(slots, rank, hidden))


def solution(mesh):
    placed = (
        P(("seq", "tp"), None),
        P("seq", "tp"),
        P("seq", None, "tp"),
        P("seq", None, "tp"),
        P("seq"),
        P("seq"),
        P(),
    )
    return jax.shard_map(
        per_device,
        mesh=mesh,
        in_specs=placed,
        out_specs=(
            P("seq", "tp"),
            P(("seq", "tp"), None),
            P("seq", None, "tp"),
            P("seq", None, "tp"),
        ),
        check_vma=False,
    )
```

profile of v0, /device:TPU:0, one launch (start us, length us, event | category | flops | bytes accessed | tf_op | source)
XLA Modules:
  0.0 90.6 jit_solution(12068702866756958323)
XLA Ops:
  1.9 1.3 %fusion.1 = s32[]{:T(128)} fusion(s32[64]{0:T(128)} %param.13, s32[]{:T(128)} %bitcast.9), kind=kLoop, calls=%fused_computation.5 | loop fusion | flops 191 | bytes 264 | tf_op jit(solution)/shard_map/reduce_sum | solution.py:350
  3.2 0.6 compare_select_fusion.1
  3.9 0.7 broadcast_in_dim.27.id_ref
  4.5 0.6 broadcast_in_dim.28.live_ref
  5.1 79.6 %shard_map.102 = (bf16[16,128]{1,0:T(8,128)(2,1)}, bf16[16,7168]{1,0:T(8,128)(2,1)}, f32[64,2048]{1,0:T(8,128)}, f32[64,7168]{1,0:T(8,128)}, bf16[64,4096]{1,0:T(8,128)(2,1)}) custom-call(bf16[64,2048]{1,0:T(8,128)(2,1)} %bitcast.14, bf16[64,7168]{1,0:T(8,128)(2,1)} %bitcast.12, bf16[64,4096]{1,0:T(8,128)(2,1)} %x_ref.1, bf16[128,7168]{1,0:T(8,128)(2,1)} %g_ref.1, ...), custom_call_target="tpu_custom_call" | custom-call | tf_op jit(solution)/shard_map/pallas_call | solution.py:305
  84.7 0.0 copy-start.2
  84.7 0.0 copy-start.1
  84.7 0.0 copy-start
  84.7 3.0 %fusion = bf16[128,7168]{1,0:T(8,128)(2,1)} fusion(bf16[16,128]{1,0:T(8,128)(2,1)} %get-tuple-element.9, bf16[16,7168]{1,0:T(8,128)(2,1)} %get-tuple-element.10), kind=kOutput, calls=%fused_computation.1 | convolution fusion | flops 31195136 | bytes 2068480 | tf_op jit(solution)/shard_map/rt,rf->tf/dot_general | solution.py:358
  87.7 0.0 copy-done.2
  87.7 0.8 copy.16
  88.5 0.0 copy-done.1
  88.5 0.8 copy.17
  89.3 0.0 copy-done
  89.3 1.2 %copy.18 = f32[4,16,7168]{2,1,0:T(8,128)} copy(f32[4,16,7168]{2,1,0:T(8,128)S(1)} %bitcast.11) | data formatting | bytes 3670016
  (1 shorter events, 0.0 us)
Async XLA Ops:
  84.7 3.0 %copy-start.2 = (bf16[64,4096]{1,0:T(8,128)(2,1)S(1)}, bf16[64,4096]{1,0:T(8,128)(2,1)}, u32[]{:S(2)}) copy-start(bf16[64,4096]{1,0:T(8,128)(2,1)} %get-tuple-element.19) | copy-start | bytes 1572868
  84.7 3.8 %copy-start.1 = (f32[64,2048]{1,0:T(8,128)S(1)}, f32[64,2048]{1,0:T(8,128)}, u32[]{:S(2)}) copy-start(f32[64,2048]{1,0:T(8,128)} %get-tuple-element.12) | copy-start | bytes 1572868
  84.7 4.6 %copy-start = (f32[64,7168]{1,0:T(8,128)S(1)}, f32[64,7168]{1,0:T(8,128)}, u32[]{:S(2)}) copy-start(f32[64,7168]{1,0:T(8,128)} %get-tuple-element.13) | copy-start | bytes 5505028
where the time goes:
time: 91 us; the launch traced here: 90.6 us
  Pallas kernels  79.6 us (87%)
  local copies, waits for them, and re-layouts  4.08 us (4%)
  matrix products  2.99 us (3%)
  between operations  1.97 us (2%)
  other arithmetic  1.95 us (2%)
    pallas_call x1, Pallas kernels, step(): pl.pallas_call(functools.partial(step_kernel, n, tp), out_shape=(jax.Shap...  79.6 us
    dot_general x1, matrix products, per_device(): jnp.einsum('rt,rf->tf', down, pick_b, preferred_element_type=f32)  2.99 us
    unnamed x9, local copies, waits for them, and re-layouts  2.83 us

commit v1 on v0

v1 whole, which is shorter than its diff:
```python
import functools

import jax
import jax.numpy as jnp
from jax import lax
from jax.experimental import pallas as pl
from jax.experimental.pallas import tpu as pltpu
from jax.sharding import PartitionSpec as P

adapter_scale = 2.0
GROUP = 4
MESH = pl.DeviceIdType.MESH
VMEM = pltpu.VMEM
SMEM = pltpu.SMEM

DOWN_FACTOR, UP_FACTOR = "Xx", "xxxxxxX"
UP_GRADIENT, DOWN_GRADIENT = "xzxzxzx", "XX"
LAG = 6


def pieces(width, most):
    tiles = width // 128
    count = max(k for k in range(1, most + 1) if tiles % k == 0)
    step = width // count
    return [(i * step, step) for i in range(count)]


def layout(width, hidden):
    out = []
    for which, size, most in (("a", width // 2, len(DOWN_FACTOR)), ("b", hidden // 2, len(UP_FACTOR))):
        base = 0 if which == "a" else width // 2
        for i, (start, step) in enumerate(pieces(size, most)):
            out.append((which, i, start, step, base + start))
    return out


def greet(n, tp, me, mine, partners):
    barrier = pltpu.get_barrier_semaphore()

    def signal(seq_at, tp_at):
        pl.semaphore_signal(barrier, inc=1, device_id=(seq_at, tp_at), device_id_type=MESH)

    for partner in partners:
        signal(partner, mine)
    for d in range(1, tp):
        signal(me, lax.rem(mine + d, tp))
    pl.semaphore_wait(barrier, len(partners) + tp - 1)


def step_kernel(
    n, tp, a_ref, b_ref, x_ref, g_ref, adapter_ref, live_ref, home_ref,
    out_ref, grad_a, grad_b, x_out,
    pick_a, pick_b, raw, chosen, land, far_land, fin, terms, spare, placed, xt, g, ids, part, gx,
    raw_send, raw_recv, hop_send, hop_recv, plane_send, plane_recv, fin_send, fin_recv,
    lead_send, lead_recv, go_send, pass_send, go_recv, cross_send, cross_recv, out_send, out_recv,
    id_send, id_recv, x_send, x_recv, part_send, part_recv, gx_send, gx_recv, local_sem,
):
    me, mine = lax.axis_index("seq"), lax.axis_index("tp")
    planes = n // GROUP
    p, spot = me // GROUP, lax.rem(me, GROUP)
    side, core = spot // 2, lax.rem(spot, 2)
    near_spot, far_spot = spot + 1 - 2 * core, spot + 2 - 4 * side
    diag_spot = far_spot + 1 - 2 * core
    first = p * GROUP
    near, far, diag = first + near_spot, first + far_spot, first + diag_spot
    rows = a_ref.shape[0]
    rank = pick_a.shape[0]
    width, hidden = pick_a.shape[1], pick_b.shape[1]
    half_a, half_b = width // 2, hidden // 2
    tokens = g.shape[0]
    slots = rows // rank
    f32, low = jnp.float32, jnp.bfloat16
    chunks = layout(width, hidden)
    count = len(chunks)

    def remote(src, dst, send, recv, seq_at, tp_at=mine):
        return pltpu.make_async_remote_copy(
            src_ref=src, dst_ref=dst, send_sem=send, recv_sem=recv,
            device_id=(seq_at, tp_at), device_id_type=MESH,
        )

    def at(index, step, size=None):
        return pl.ds(pl.multiple_of(index * step, step), step if size is None else size)

    def half_cols(chunk, which_half):
        which, _, start, size, _ = chunk
        half = half_a if which == "a" else half_b
        return pl.ds(pl.multiple_of(which_half * half + start, 128), size)

    def span(chunk):
        return pl.ds(chunk[4], chunk[3])

    def when(cond, body):
        if cond is True:
            body()
        else:
            pl.when(cond)(body)

    pending = []
    tick = [0]

    def send(copy, cond=True):
        copy.start()
        pending.append((tick[0], cond, copy))

    def drain(before):
        while pending and pending[0][0] < before:
            _, cond, copy = pending.pop(0)
            when(cond, copy.wait_send)

    local = [
        pltpu.make_async_copy(a_ref.at[:, at(core, half_a)], raw.at[at(spot, rows), pl.ds(0, half_a)], local_sem.at[0]),
        pltpu.make_async_copy(b_ref.at[:, at(core, half_b)], raw.at[at(spot, rows), pl.ds(half_a, half_b)], local_sem.at[1]),
        pltpu.make_async_copy(x_ref.at[:, at(mine, width)], xt.at[mine], local_sem.at[2]),
        pltpu.make_async_copy(g_ref, g, local_sem.at[3]),
    ]
    for copy in local:
        copy.start()
    adapter = adapter_ref[0]
    home = home_ref[adapter]
    id_row = lax.broadcasted_iota(jnp.int32, ids.shape[1:], 0)
    ids[me] = jnp.where(id_row == 0, adapter, home)
    others = [lax.rem(p + d, planes) for d in range(1, planes)]
    greet(n, tp, me, mine, [near, far, diag] + [q * GROUP + spot for q in others])
    for partner in (near, far, diag):
        send(remote(ids.at[me], ids.at[me], id_send.at[0], id_recv.at[planes], partner))
    pending.clear()

    factor_kind = [DOWN_FACTOR[i] if w == "a" else UP_FACTOR[i] for w, i, *_ in chunks]
    term_kind = [DOWN_GRADIENT[i] if w == "a" else UP_GRADIENT[i] for w, i, *_ in chunks]

    def x_first(kind):
        return kind in "xX"

    def relayed(kind):
        return kind in "xz"

    pairs = planes // 2
    pair = p // 2
    partner = p + 1 - 2 * lax.rem(p, 2)
    other_pairs = [lax.rem(pair + d, pairs) for d in range(1, pairs)]

    def inner(other):
        return 2 * other + (other < pair).astype(jnp.int32)

    def seat(plane):
        return plane * GROUP + spot

    def factor(chunk):
        return a_ref if chunk[0] == "a" else b_ref

    def picked(chunk):
        return pick_a if chunk[0] == "a" else pick_b

    raw_copies = {}

    def raw_out(j):
        chunk = chunks[j]
        own, sp = at(spot, rows), span(chunk)
        there, here = factor(chunk).at[:, half_cols(chunk, 1 - core)], factor(chunk).at[:, half_cols(chunk, core)]
        routes = [(there, near), (here, far), (there, diag)][:3 if x_first(factor_kind[j]) else 1]
        for src, to in routes:
            remote(src, raw.at[own, sp], raw_send.at[j], raw_recv.at[j], to).start()
        everything = raw.at[pl.ds(0, len(routes) * rows), sp]
        raw_copies[j] = remote(everything, everything, raw_send.at[j], raw_recv.at[j], near)
        pending.append((tick[0], True, raw_copies[j]))

    for j in range(min(4, count)):
        raw_out(j)
    x_copies = []
    for d in range(1, tp):
        peer = lax.rem(mine + d, tp)
        x_copies.append(remote(x_ref.at[:, at(peer, width)], xt.at[mine], x_send.at[d], x_recv.at[d], me, peer))
        x_copies[-1].start()
    for copy in local:
        copy.wait()
    plane_ids = ids.at[pl.ds(first, GROUP - 1)]
    remote(plane_ids, plane_ids, id_send.at[0], id_recv.at[planes], near).wait()

    def id_hop(source, to, sends):
        block = ids.at[at(source, GROUP)]
        return remote(block, block, sends, id_recv.at[source], to)

    for q in others:
        id_hop(p, q * GROUP + spot, id_send.at[1]).start()
    for q in others:
        id_hop(q, near, id_send.at[1]).wait_recv()
    other_ids = ids.at[pl.ds(0, GROUP * (planes - 1))]
    remote(other_ids, other_ids, id_send.at[1], id_recv.at[0], near).wait_send()

    def wanted(block, which, shape):
        return jnp.broadcast_to(ids[block, which:which + 1, 0:1], shape)

    def selector(spots, base, depth):
        shape = (rank, depth)
        row_at, col_at = lax.broadcasted_iota(jnp.int32, shape, 0), lax.broadcasted_iota(jnp.int32, shape, 1)
        found = []
        for q in range(planes):
            for s in spots:
                local_id = wanted(q * GROUP + s, 0, shape) - base
                found.append((col_at == local_id * rank + row_at).astype(f32))
        return jnp.concatenate(found, axis=0).astype(low)

    pick_x = selector([side * 2, side * 2 + 1], first * slots, GROUP * rows)
    pick_z = selector(list(range(GROUP)), (first + side * 2) * slots, 2 * rows)

    def placement(owner):
        shape = (rows, n * rank)
        row_at, col_at = lax.broadcasted_iota(jnp.int32, shape, 0), lax.broadcasted_iota(jnp.int32, shape, 1)
        target = jnp.full(shape, -1, jnp.int32)
        for block in range(n):
            begin = block * rank
            here = (wanted(block, 1, shape) - owner * slots) * rank + col_at - begin
            target = jnp.where((col_at >= begin) & (col_at < begin + rank), here, target)
        return (target == row_at).astype(f32).astype(low)

    place = jnp.concatenate([placement(me), placement(near)], axis=0)

    def factor_rows(j):
        return 2 * rank if x_first(factor_kind[j]) else GROUP * rank

    def select(j):
        sp, kind = span(chunks[j]), factor_kind[j]
        if j + 4 < count:
            raw_out(j + 4)
        raw_copies[j].wait_recv()
        if x_first(kind):
            got = jnp.dot(pick_x, raw[:, sp], preferred_element_type=f32)
        else:
            got = jnp.dot(pick_z, raw[at(side, 2 * rows), sp], preferred_element_type=f32)
        depth = factor_rows(j)
        chosen[:, pl.ds(0, depth), sp] = got.astype(low).reshape(planes, depth, got.shape[1])

    def each_plane(body):
        for v in range(planes):
            pl.when(p == v)(functools.partial(body, v))

    def beyond(v):
        return pl.ds(v + 1, planes - 1 - v) if v % 2 == 0 else pl.ds(0, v)

    def plane_copies(j, count):
        block = far_land.at[pl.ds(0, count), pl.ds(0, factor_rows(j)), span(chunks[j])]
        return remote(block, block, plane_send.at[j], plane_recv.at[j], near)

    def send_plane(j, q):
        rest, sp = pl.ds(0, factor_rows(j)), span(chunks[j])
        remote(chosen.at[q, rest, sp], far_land.at[p, rest, sp], plane_send.at[j], plane_recv.at[j], seat(q)).start()

    def hop(j):
        if not relayed(factor_kind[j]):
            for q in others:
                send_plane(j, q)
            pending.append((tick[0], True, plane_copies(j, planes - 1)))
            return
        rest, sp = pl.ds(0, factor_rows(j)), span(chunks[j])

        def copy(v):
            part_of = beyond(v)
            return remote(
                chosen.at[part_of, rest, sp], land.at[part_of, rest, sp], hop_send.at[j], hop_recv.at[j], seat(partner)
            )

        each_plane(lambda v: copy(v).start())
        for v in range(planes):
            pending.append((tick[0], p == v, copy(v)))

    def relay(j):
        if not relayed(factor_kind[j]):
            return
        rest, sp = pl.ds(0, factor_rows(j)), span(chunks[j])

        def body(v):
            got = pl.ds(v, planes - v) if v % 2 else pl.ds(0, v + 1)
            here = land.at[got, rest, sp]
            remote(here, here, hop_send.at[j], hop_recv.at[j], near).wait_recv()
            chosen[got, rest, sp] = chosen[got, rest, sp] + land[got, rest, sp]
            for q in range(v + 1, planes) if v % 2 else range(v):
                send_plane(j, q)

        each_plane(body)
        for v in range(planes):
            sent = planes - 1 - v if v % 2 else v
            if sent:
                pending.append((tick[0], p == v, plane_copies(j, sent)))

    fin_copies = {}

    def final(j):
        chunk, depth = chunks[j], factor_rows(j)
        sp = span(chunk)
        rest = pl.ds(0, depth)
        sources = [inner(other) for other in other_pairs] if relayed(factor_kind[j]) else others
        if sources:
            plane_copies(j, len(sources)).wait_recv()
            total = chosen[p, rest, sp]
            for q in sources:
                total = total + far_land[q, rest, sp]
            chosen[p, rest, sp] = total
        target = picked(chunk)
        mine_cols = half_cols(chunk, core)
        if x_first(factor_kind[j]):
            fin_copies[j] = remote(
                chosen.at[p, at(1 - core, rank), sp], target.at[:, mine_cols], fin_send.at[j], fin_recv.at[j], near
            )
            fin_copies[j].start()
            target[:, mine_cols] = chosen[p, at(core, rank), sp]
        else:
            for k, (peer, peer_spot) in enumerate(((near, near_spot), (far, far_spot), (diag, diag_spot))):
                remote(chosen.at[p, at(peer_spot, rank), sp], fin.at[k, :, sp], fin_send.at[j], fin_recv.at[j], peer).start()
            fin_copies[j] = remote(fin.at[:, :, sp], fin.at[:, :, sp], fin_send.at[j], fin_recv.at[j], near)
        pending.append((tick[0], True, fin_copies[j]))

    def settle(j):
        chunk = chunks[j]
        sp = span(chunk)
        fin_copies[j].wait_recv()
        if not x_first(factor_kind[j]):
            target = picked(chunk)
            target[:, half_cols(chunk, core)] = chosen[p, at(spot, rank), sp] + fin[1, :, sp]
            target[:, half_cols(chunk, 1 - core)] = fin[0, :, sp] + fin[2, :, sp]

    def outer(left, right):
        return lax.dot_general(left, right, (((1,), (1,)), ((), ())), preferred_element_type=f32)

    part_copies = []
    lane = lax.broadcasted_iota(jnp.int32, (1, tokens), 1)
    alive = (lane < live_ref[0]).astype(f32)

    def share(which, value):
        part[which, 0] = value
        for d in range(1, tp):
            copy = remote(
                part.at[which, 0], part.at[which, d], part_send.at[which, d], part_recv.at[which, d],
                me, lax.rem(mine + d, tp),
            )
            send(copy)
            part_copies.append(copy)

    def collect(which):
        value = part[which, 0]
        for d in range(1, tp):
            part_copies[which * (tp - 1) + d - 1].wait_recv()
            value = value + part[which, d]
        return value * alive

    lead_copies = {}

    def lead(j, left, right, scale):
        chunk = chunks[j]
        sp, own = span(chunk), at(me, rank)

        def term(which_half):
            value = jnp.dot(left, right(half_cols(chunk, which_half)), preferred_element_type=f32)
            return (scale * value if scale is not None else value).astype(low)

        spare[:, sp] = term(1 - core)
        remote(spare.at[:, sp], terms.at[own, sp], lead_send.at[j], lead_recv.at[j], near).start()
        if not x_first(term_kind[j]):
            remote(spare.at[:, sp], terms.at[own, sp], lead_send.at[j], lead_recv.at[j], diag).start()
        terms[own, sp] = term(core)
        if not x_first(term_kind[j]):
            remote(terms.at[own, sp], terms.at[own, sp], lead_send.at[j], lead_recv.at[j], far).start()
        everything = terms.at[pl.ds(0, (1 if x_first(term_kind[j]) else GROUP - 1) * rank), sp]
        lead_copies[j] = remote(everything, everything, lead_send.at[j], lead_recv.at[j], near)
        pending.append((tick[0], True, lead_copies[j]))

    def group_rows(j, plane, other_side=False):
        if not x_first(term_kind[j]):
            return at(plane, GROUP * rank)
        return at(plane * 2 + (1 - side if other_side else side), 2 * rank)

    def term_copy(j, plane, sends, to):
        block = terms.at[group_rows(j, plane), span(chunks[j])]
        return remote(block, block, sends.at[j], go_recv.at[j, plane], to)

    def cross_copy(j, plane):
        block = terms.at[group_rows(j, plane), span(chunks[j])]
        return remote(block, block, cross_send.at[j], cross_recv.at[j], far)

    def crossed(j):
        everything = terms.at[pl.ds(0, planes * 2 * rank), span(chunks[j])]
        return remote(everything, everything, cross_send.at[j], cross_recv.at[j], far)

    def spread(j):
        lead_copies[j].wait_recv()
        targets = [partner] + [inner(other) for other in other_pairs] if relayed(term_kind[j]) else others
        for q in targets:
            term_copy(j, p, go_send, seat(q)).start()
        if x_first(term_kind[j]):
            cross_copy(j, p).start()
        pending.append((tick[0], True, term_copies(j, go_send, len(targets))))

    def term_copies(j, sends, number):
        block = terms.at[pl.ds(0, number * (2 if x_first(term_kind[j]) else GROUP) * rank), span(chunks[j])]
        return remote(block, block, sends.at[j], go_recv.at[j, 0], near)

    def arrive(j, q):
        term_copy(j, q, go_send, near).wait_recv()
        if x_first(term_kind[j]):
            cross_copy(j, q).start()

    def pass_on(j):
        if not relayed(term_kind[j]):
            for q in others:
                arrive(j, q)
            return
        arrive(j, partner)

        def body(v):
            for q in range(v) if v % 2 == 0 else range(planes - 1, v, -1):
                term_copy(j, q, go_send, near).wait_recv()
                term_copy(j, q, pass_send, seat(partner)).start()
                if x_first(term_kind[j]):
                    cross_copy(j, q).start()

        each_plane(body)
        for v in range(planes):
            passed = v if v % 2 == 0 else planes - 1 - v
            if passed:
                pending.append((tick[0], p == v, term_copies(j, pass_send, passed)))

    def gather(j):
        if relayed(term_kind[j]):

            def body(v):
                for q in range(v + 2, planes) if v % 2 == 0 else range(v - 2, -1, -1):
                    arrive(j, q)

            each_plane(body)
        if x_first(term_kind[j]):
            pending.append((tick[0], True, crossed(j)))

    out_copies = {}

    def finish(j):
        chunk = chunks[j]
        sp, cols = span(chunk), half_cols(chunk, core)
        if x_first(term_kind[j]):
            crossed(j).wait_recv()
        out = grad_a if chunk[0] == "a" else grad_b
        total = jnp.dot(place, terms[:, sp], preferred_element_type=f32)
        placed[:, sp] = total[rows:]
        out_copies[j] = remote(placed.at[:, sp], out.at[:, cols], out_send.at[j], out_recv.at[j], near)
        send(out_copies[j])
        out[:, cols] = total[:rows]

    state = {}

    def start_down():
        for copy in x_copies:
            copy.wait()
        share(0, outer(pick_a[...], xt[...].reshape(tokens, width)))

    def finish_down():
        down = collect(0).astype(low)
        state["down"] = down
        state["down_t"] = down.T

    def add_back(j):
        total = state.get("back")
        for h in (core, 1 - core):
            cols = half_cols(chunks[j], h)
            value = outer(pick_b[:, cols], g[:, cols])
            total = value if total is None else total + value
        state["back"] = total

    def output(j):
        for h in (core, 1 - core):
            cols = half_cols(chunks[j], h)
            value = jnp.dot(state["down_t"], pick_b[:, cols], preferred_element_type=f32)
            out_ref[:, cols] = (adapter_scale * value).astype(low)

    def start_back():
        share(1, state["back"])

    gx_copies = []

    def finish_back():
        back = adapter_scale * collect(1)
        state["back_low"] = back.astype(low)
        state["back_t"] = back.T.astype(low)

    def input_gradient():
        gx[...] = jnp.dot(state["back_t"], pick_a[...], preferred_element_type=f32).astype(low).reshape(gx.shape)
        for d in range(1, tp):
            peer = lax.rem(mine + d, tp)
            gx_copies.append(remote(gx.at[peer], x_out.at[:, at(mine, width)], gx_send.at[d], gx_recv.at[d], me, peer))
            gx_copies[-1].start()
        x_out[:, at(mine, width)] = gx[mine]

    events = []

    def plan(when_at, order, body):
        events.append((when_at, order, len(events), body))

    downs = [j for j in range(count) if chunks[j][0] == "a"]
    ups = [j for j in range(count) if chunks[j][0] == "b"]
    for j in range(count):
        plan(j, 5, functools.partial(select, j))
        plan(j, 5, functools.partial(hop, j))
        plan(j + 1, 4, functools.partial(relay, j))
        plan(j + 2, 3, functools.partial(final, j))
        plan(j + 3, 2, functools.partial(settle, j))
        if j in ups:
            plan(j + 3, 2, functools.partial(add_back, j))
    ready = downs[-1] + 3
    plan(ready, 2, start_down)
    plan(ready + 1, 1, finish_down)

    def chain(j, begin, left, right, scale):
        plan(begin, 6, lambda: lead(j, state[left], right, scale))
        plan(begin + 1, 7, functools.partial(spread, j))
        plan(begin + 2, 8, functools.partial(pass_on, j))
        plan(begin + 3, 9, functools.partial(gather, j))
        plan(begin + 4, 10, functools.partial(finish, j))

    for i, j in enumerate(ups):
        plan(max(ready + 1, j + 3) + 2, 11, functools.partial(output, j))
        chain(j, ready + 1 + i, "down", lambda cols: g[:, cols], adapter_scale)
    whole = ups[-1] + 3
    plan(whole, 2, start_back)
    plan(whole + 1, 1, finish_back)
    for i, j in enumerate(downs):
        chain(j, whole + 1, "back_low", lambda cols: xt[:, :, cols].reshape(tokens, cols.size), None)
    plan(whole + 1, 12, input_gradient)
    for when_at, _, _, body in sorted(events, key=lambda event: event[:3]):
        if when_at != tick[0]:
            tick[0] = when_at
            drain(when_at - LAG)
        body()
    for j in ups + downs:
        out_copies[j].wait_recv()
    for copy in gx_copies:
        copy.wait()
    drain(tick[0] + 1)


def step(n, tp, a, b, x, g, adapter, live, home):
    slots, rank, width = a.shape
    hidden = b.shape[2]
    rows = x.shape[0]
    tokens = g.shape[0]
    planes = n // GROUP
    cuts = len(layout(width, hidden))
    own = slots * rank
    each = (width + hidden) // 2
    low, f32 = jnp.bfloat16, jnp.float32
    dma = pltpu.SemaphoreType.DMA
    hbm = pl.BlockSpec(memory_space=pltpu.HBM)
    inside = pl.BlockSpec(memory_space=VMEM)
    scalar = pl.BlockSpec(memory_space=SMEM)
    lists = [dma((cuts,)) for _ in range(12)]
    results = ((tokens, hidden), low), ((own, width), f32), ((own, hidden), f32), ((rows, tp * width), low)
    held = pl.pallas_call(
        functools.partial(step_kernel, n, tp),
        out_shape=tuple(VMEM(*result) for result in results),
        in_specs=[hbm] * 4 + [scalar] * 3,
        out_specs=(inside,) * 4,
        scratch_shapes=[
            VMEM((rank, width), low), VMEM((rank, hidden), low), VMEM((GROUP * own, each), low),
            VMEM((planes, GROUP * rank, each), low),
            VMEM((planes, GROUP * rank, each), low), VMEM((planes, GROUP * rank, each), low),
            VMEM((3, rank, each), low), VMEM((n * rank, each), low), VMEM((rank, each), low), VMEM((own, each), f32),
            VMEM((tp, rows, width), low), VMEM((tokens, hidden), low),
            VMEM((n, 2, 128), jnp.int32), VMEM((2, tp, rank, tokens), f32), VMEM((tp, rows, width), low),
            *lists, dma((cuts, planes)), dma((cuts,)), dma((cuts,)), dma((cuts,)), dma((cuts,)),
            dma((3,)), dma((planes + 1,)), dma((tp,)), dma((tp,)), dma((2, tp)), dma((2, tp)),
            dma((tp,)), dma((tp,)), dma((4,)),
        ],
        compiler_params=pltpu.CompilerParams(
            collective_id=0, has_side_effects=True, vmem_limit_bytes=56 * 1024 * 1024
        ),
    )(a.reshape(own, width), b.reshape(own, hidden), x, g, adapter, live, home)
    return held


def per_device(
    normed_input,
    output_gradient,
    adapter_down,
    adapter_up,
    adapter_of_block,
    live_per_block,
    adapter_home_row,
):
    n, tp = lax.axis_size("seq"), lax.axis_size("tp")
    slots, rank, width = adapter_down.shape
    hidden = adapter_up.shape[2]
    out, grad_a, grad_b, gx = step(
        n, tp, adapter_down, adapter_up, normed_input, output_gradient,
        adapter_of_block, live_per_block, adapter_home_row,
    )
    return (out, gx, grad_a.reshape(slots, rank, width), grad_b.reshape(slots, rank, hidden))


def solution(mesh):
    placed = (
        P(("seq", "tp"), None),
        P("seq", "tp"),
        P("seq", None, "tp"),
        P("seq", None, "tp"),
        P("seq"),
        P("seq"),
        P(),
    )
    return jax.shard_map(
        per_device,
        mesh=mesh,
        in_specs=placed,
        out_specs=(
            P("seq", "tp"),
            P(("seq", "tp"), None),
            P("seq", None, "tp"),
            P("seq", None, "tp"),
        ),
        check_vma=False,
    )
```

time: 91 us -> 82.4 us (0.905)
  Pallas kernels: 79.6 us -> 76.3 us
  matrix products: 2.99 us -> 0 us
  other arithmetic: 1.95 us -> 0 us
    pallas_call x1, Pallas kernels: 79.6 us -> 76.3 us  [step(): pl.pallas_call(functools.partial(step_kernel, n, tp), out_shape=tuple((VM...]
    dot_general x1 -> x0, matrix products: 2.99 us -> none  [per_device(): jnp.einsum('rt,rf->tf', down, pick_b, preferred_element_type=f32)]
    reduce_sum x1 -> x0, other arithmetic: 1.29 us -> none  [per_device(): jnp.sum(jnp.where(jnp.arange(adapters, dtype=jnp.int32) == adapter, adapt...]
    broadcast_in_dim x2 -> x0, local copies, waits for them, and re-layouts: 1.25 us -> none  [the longest x1 0.66 us: per_device(): ids = jnp.broadcast_to(ids, (8, 128))]
    unnamed x9 -> x4, local copies, waits for them, and re-layouts: 2.83 us -> 4.04 us
where the time goes in v1:
time: 82.4 us; the launch traced here: 82.3 us
  Pallas kernels  76.3 us (93%)
  local copies, waits for them, and re-layouts  4.04 us (5%)
  between operations  1.93 us (2%)
    pallas_call x1, Pallas kernels, step(): pl.pallas_call(functools.partial(step_kernel, n, tp), out_shape=tuple((VM...  76.3 us
    unnamed x4, local copies, waits for them, and re-layouts  4.04 us

profile of v1, /device:TPU:0, one launch (start us, length us, event | category | flops | bytes accessed | tf_op | source)
XLA Modules:
  0.0 82.3 jit_solution(100306003926376298)
XLA Ops:
  1.9 76.3 %shard_map.102 = (bf16[128,7168]{1,0:T(8,128)(2,1)S(1)}, f32[64,2048]{1,0:T(8,128)S(1)}, f32[64,7168]{1,0:T(8,128)S(1)}, bf16[64,4096]{1,0:T(8,128)(2,1)S(1)}) custom-call(bf16[64,2048]{1,0:T(8,128)(2,1)} %bitcast.7, bf16[64,7168]{1,0:T(8,128)(2,1)} %bitcast.6, bf16[64,4096]{1,0:T(8,128)(2,1)} %x_ref.1, bf16[128,7168]{1,0:T(8,128)(2,1)} %g_ref.1, ...), custom_call_target="tpu_custom_call" | custom-call | tf_op jit(solution)/shard_map/pallas_call | solution.py:554
  78.2 1.2 %copy.15 = bf16[128,7168]{1,0:T(8,128)(2,1)} copy(bf16[128,7168]{1,0:T(8,128)(2,1)S(1)} %get-tuple-element.12) | data formatting | bytes 3670016
  79.5 0.8 copy.16
  80.2 0.8 copy.17
  81.0 1.2 %copy.18 = f32[4,16,7168]{2,1,0:T(8,128)} copy(f32[4,16,7168]{2,1,0:T(8,128)S(1)} %bitcast.4) | data formatting | bytes 3670016

commit v2 on v1

--- a/solution.py
+++ b/solution.py
@@ -13,9 +13,10 @@
 VMEM = pltpu.VMEM
 SMEM = pltpu.SMEM
 
-DOWN_FACTOR, UP_FACTOR = "Xx", "xxxxxxX"
-UP_GRADIENT, DOWN_GRADIENT = "xzxzxzx", "XX"
-LAG = 6
+DOWN_FACTOR, UP_FACTOR = "XX", "xxxxxxX"
+UP_GRADIENT, DOWN_GRADIENT = "xxxxxxX", "XZ"
+RELAY, LAND, NEAR, SHARE, LEAD, SPREAD, CROSS = 2, 2, 1, 1, 1, 2, 1
+AHEAD, LAG = 4, 6
 
 
 def pieces(width, most):
@@ -165,7 +166,7 @@
         raw_copies[j] = remote(everything, everything, raw_send.at[j], raw_recv.at[j], near)
         pending.append((tick[0], True, raw_copies[j]))
 
-    for j in range(min(4, count)):
+    for j in range(min(AHEAD, count)):
         raw_out(j)
     x_copies = []
     for d in range(1, tp):
@@ -221,8 +222,8 @@
 
     def select(j):
         sp, kind = span(chunks[j]), factor_kind[j]
-        if j + 4 < count:
-            raw_out(j + 4)
+        if j + AHEAD < count:
+            raw_out(j + AHEAD)
         raw_copies[j].wait_recv()
         if x_first(kind):
             got = jnp.dot(pick_x, raw[:, sp], preferred_element_type=f32)
@@ -495,34 +496,42 @@
 
     downs = [j for j in range(count) if chunks[j][0] == "a"]
     ups = [j for j in range(count) if chunks[j][0] == "b"]
+    def settled_at(j):
+        return j + (RELAY + LAND if relayed(factor_kind[j]) else LAND) + NEAR
+
     for j in range(count):
         plan(j, 5, functools.partial(select, j))
         plan(j, 5, functools.partial(hop, j))
-        plan(j + 1, 4, functools.partial(relay, j))
-        plan(j + 2, 3, functools.partial(final, j))
-        plan(j + 3, 2, functools.partial(settle, j))
+        plan(j + RELAY, 4, functools.partial(relay, j))
+        plan(settled_at(j) - NEAR, 3, functools.partial(final, j))
+        plan(settled_at(j), 2, functools.partial(settle, j))
         if j in ups:
-            plan(j + 3, 2, functools.partial(add_back, j))
-    ready = downs[-1] + 3
+            plan(settled_at(j), 2, functools.partial(add_back, j))
+    ready = max(settled_at(j) for j in downs)
     plan(ready, 2, start_down)
-    plan(ready + 1, 1, finish_down)
+    plan(ready + SHARE, 1, finish_down)
 
     def chain(j, begin, left, right, scale):
         plan(begin, 6, lambda: lead(j, state[left], right, scale))
-        plan(begin + 1, 7, functools.partial(spread, j))
-        plan(begin + 2, 8, functools.partial(pass_on, j))
-        plan(begin + 3, 9, functools.partial(gather, j))
-        plan(begin + 4, 10, functools.partial(finish, j))
+        arrived = begin + LEAD + SPREAD
+        plan(begin + LEAD, 7, functools.partial(spread, j))
+        plan(arrived, 8, functools.partial(pass_on, j))
+        if relayed(term_kind[j]):
+            arrived += SPREAD
+        plan(arrived, 9, functools.partial(gather, j))
+        if x_first(term_kind[j]):
+            arrived += CROSS
+        plan(arrived, 10, functools.partial(finish, j))
 
     for i, j in enumerate(ups):
-        plan(max(ready + 1, j + 3) + 2, 11, functools.partial(output, j))
-        chain(j, ready + 1 + i, "down", lambda cols: g[:, cols], adapter_scale)
-    whole = ups[-1] + 3
+        plan(max(ready + SHARE, settled_at(j)) + 2, 11, functools.partial(output, j))
+        chain(j, ready + SHARE + i, "down", lambda cols: g[:, cols], adapter_scale)
+    whole = max(settled_at(j) for j in ups)
     plan(whole, 2, start_back)
-    plan(whole + 1, 1, finish_back)
+    plan(whole + SHARE, 1, finish_back)
     for i, j in enumerate(downs):
-        chain(j, whole + 1, "back_low", lambda cols: xt[:, :, cols].reshape(tokens, cols.size), None)
-    plan(whole + 1, 12, input_gradient)
+        chain(j, whole + SHARE, "back_low", lambda cols: xt[:, :, cols].reshape(tokens, cols.size), None)
+    plan(whole + SHARE, 12, input_gradient)
     for when_at, _, _, body in sorted(events, key=lambda event: event[:3]):
         if when_at != tick[0]:
             tick[0] = when_at

time: 82.4 us -> 70.4 us (0.85)
  Pallas kernels: 76.3 us -> 64.3 us
    pallas_call x1, Pallas kernels: 76.3 us -> 64.3 us  [step(): pl.pallas_call(functools.partial(step_kernel, n, tp), out_shape=tuple((VM...]
where the time goes in v2:
time: 70.4 us; the launch traced here: 70.3 us
  Pallas kernels  64.3 us (91%)
  local copies, waits for them, and re-layouts  4.04 us (6%)
  between operations  1.93 us (3%)
    pallas_call x1, Pallas kernels, step(): pl.pallas_call(functools.partial(step_kernel, n, tp), out_shape=tuple((VM...  64.3 us
    unnamed x4, local copies, waits for them, and re-layouts  4.04 us

profile of v2, /device:TPU:0, one launch (start us, length us, event | category | flops | bytes accessed | tf_op | source)
XLA Modules:
  0.0 70.3 jit_solution(14746197544322644312)
XLA Ops:
  1.9 64.3 %shard_map.102 = (bf16[128,7168]{1,0:T(8,128)(2,1)S(1)}, f32[64,2048]{1,0:T(8,128)S(1)}, f32[64,7168]{1,0:T(8,128)S(1)}, bf16[64,4096]{1,0:T(8,128)(2,1)S(1)}) custom-call(bf16[64,2048]{1,0:T(8,128)(2,1)} %bitcast.7, bf16[64,7168]{1,0:T(8,128)(2,1)} %bitcast.6, bf16[64,4096]{1,0:T(8,128)(2,1)} %x_ref.1, bf16[128,7168]{1,0:T(8,128)(2,1)} %g_ref.1, ...), custom_call_target="tpu_custom_call" | custom-call | tf_op jit(solution)/shard_map/pallas_call | solution.py:563
  66.2 1.2 %copy.15 = bf16[128,7168]{1,0:T(8,128)(2,1)} copy(bf16[128,7168]{1,0:T(8,128)(2,1)S(1)} %get-tuple-element.12) | data formatting | bytes 3670016
  67.5 0.8 %copy.16 = bf16[64,4096]{1,0:T(8,128)(2,1)} copy(bf16[64,4096]{1,0:T(8,128)(2,1)S(1)} %get-tuple-element.13) | data formatting | bytes 1048576
  68.3 0.8 %copy.17 = f32[4,16,2048]{2,1,0:T(8,128)} copy(f32[4,16,2048]{2,1,0:T(8,128)S(1)} %bitcast.5) | data formatting | bytes 1048576
  69.0 1.2 %copy.18 = f32[4,16,7168]{2,1,0:T(8,128)} copy(f32[4,16,7168]{2,1,0:T(8,128)S(1)} %bitcast.4) | data formatting | bytes 3670016

commit v3 on v2

--- a/solution.py
+++ b/solution.py
@@ -16,7 +16,8 @@
 DOWN_FACTOR, UP_FACTOR = "XX", "xxxxxxX"
 UP_GRADIENT, DOWN_GRADIENT = "xxxxxxX", "XZ"
 RELAY, LAND, NEAR, SHARE, LEAD, SPREAD, CROSS = 2, 2, 1, 1, 1, 2, 1
-AHEAD, LAG = 4, 6
+AHEAD, LAG = 4, 45
+SCHEDULE = ()
 
 
 def pieces(width, most):
@@ -491,8 +492,8 @@
 
     events = []
 
-    def plan(when_at, order, body):
-        events.append((when_at, order, len(events), body))
+    def plan(when_at, order, body, stage, j=0):
+        events.append((when_at, order, len(events), stage * 100 + j, body))
 
     downs = [j for j in range(count) if chunks[j][0] == "a"]
     ups = [j for j in range(count) if chunks[j][0] == "b"]
@@ -500,43 +501,47 @@
         return j + (RELAY + LAND if relayed(factor_kind[j]) else LAND) + NEAR
 
     for j in range(count):
-        plan(j, 5, functools.partial(select, j))
-        plan(j, 5, functools.partial(hop, j))
-        plan(j + RELAY, 4, functools.partial(relay, j))
-        plan(settled_at(j) - NEAR, 3, functools.partial(final, j))
-        plan(settled_at(j), 2, functools.partial(settle, j))
+        plan(j, 5, functools.partial(select, j), 0, j)
+        plan(j, 5, functools.partial(hop, j), 1, j)
+        plan(j + RELAY, 4, functools.partial(relay, j), 2, j)
+        plan(settled_at(j) - NEAR, 3, functools.partial(final, j), 3, j)
+        plan(settled_at(j), 2, functools.partial(settle, j), 4, j)
         if j in ups:
-            plan(settled_at(j), 2, functools.partial(add_back, j))
+            plan(settled_at(j), 2, functools.partial(add_back, j), 5, j)
     ready = max(settled_at(j) for j in downs)
-    plan(ready, 2, start_down)
-    plan(ready + SHARE, 1, finish_down)
+    plan(ready, 2, start_down, 12)
+    plan(ready + SHARE, 1, finish_down, 13)
 
     def chain(j, begin, left, right, scale):
-        plan(begin, 6, lambda: lead(j, state[left], right, scale))
+        plan(begin, 6, lambda: lead(j, state[left], right, scale), 6, j)
         arrived = begin + LEAD + SPREAD
-        plan(begin + LEAD, 7, functools.partial(spread, j))
-        plan(arrived, 8, functools.partial(pass_on, j))
+        plan(begin + LEAD, 7, functools.partial(spread, j), 7, j)
+        plan(arrived, 8, functools.partial(pass_on, j), 8, j)
         if relayed(term_kind[j]):
             arrived += SPREAD
-        plan(arrived, 9, functools.partial(gather, j))
+        plan(arrived, 9, functools.partial(gather, j), 9, j)
         if x_first(term_kind[j]):
             arrived += CROSS
-        plan(arrived, 10, functools.partial(finish, j))
+        plan(arrived, 10, functools.partial(finish, j), 10, j)
 
     for i, j in enumerate(ups):
-        plan(max(ready + SHARE, settled_at(j)) + 2, 11, functools.partial(output, j))
+        plan(max(ready + SHARE, settled_at(j)) + 2, 11, functools.partial(output, j), 11, j)
         chain(j, ready + SHARE + i, "down", lambda cols: g[:, cols], adapter_scale)
     whole = max(settled_at(j) for j in ups)
-    plan(whole, 2, start_back)
-    plan(whole + SHARE, 1, finish_back)
+    plan(whole, 2, start_back, 14)
+    plan(whole + SHARE, 1, finish_back, 15)
     for i, j in enumerate(downs):
         chain(j, whole + SHARE, "back_low", lambda cols: xt[:, :, cols].reshape(tokens, cols.size), None)
-    plan(whole + SHARE, 12, input_gradient)
-    for when_at, _, _, body in sorted(events, key=lambda event: event[:3]):
-        if when_at != tick[0]:
-            tick[0] = when_at
-            drain(when_at - LAG)
-        body()
+    plan(whole + SHARE, 12, input_gradient, 16)
+    rank_of = {code: i for i, code in enumerate(SCHEDULE)}
+    if set(rank_of) == {event[3] for event in events}:
+        events.sort(key=lambda event: rank_of[event[3]])
+    else:
+        events.sort(key=lambda event: event[:3])
+    for i, event in enumerate(events):
+        tick[0] = i
+        drain(i - LAG)
+        event[4]()
     for j in ups + downs:
         out_copies[j].wait_recv()
     for copy in gx_copies:
@@ -580,7 +585,25 @@
             collective_id=0, has_side_effects=True, vmem_limit_bytes=56 * 1024 * 1024
         ),
     )(a.reshape(own, width), b.reshape(own, hidden), x, g, adapter, live, home)
-    return held
+    anywhere = pl.BlockSpec(memory_space=pl.ANY)
+    return pl.pallas_call(
+        store_kernel,
+        out_shape=tuple(jax.ShapeDtypeStruct(*result) for result in results),
+        in_specs=[inside] * len(results),
+        out_specs=(anywhere,) * len(results),
+        scratch_shapes=[dma((len(results),))],
+        compiler_params=pltpu.CompilerParams(vmem_limit_bytes=1024 * 1024),
+    )(*[pltpu.with_memory_space_constraint(value, VMEM) for value in held])
+
+
+def store_kernel(*refs):
+    sems = refs[-1]
+    number = len(refs) // 2
+    copies = [pltpu.make_async_copy(refs[i], refs[number + i], sems.at[i]) for i in range(number)]
+    for copy in copies:
+        copy.start()
+    for copy in copies:
+        copy.wait()
 
 
 def per_device(

time: 70.4 us -> 68.6 us (0.974)
  local copies, waits for them, and re-layouts: 4.04 us -> 0 us
  Pallas kernels: 64.3 us -> 66.5 us
    unnamed x4 -> x0, local copies, waits for them, and re-layouts: 4.04 us -> none
    pallas_call x0 -> x1, Pallas kernels: none -> 2.21 us  [step(): pl.pallas_call(store_kernel, out_shape=tuple((jax.ShapeDtypeStruct(*resul...]
where the time goes in v3:
time: 68.6 us; the launch traced here: 68.4 us
  Pallas kernels  66.5 us (97%)
  between operations  1.93 us (3%)
    pallas_call x1, Pallas kernels, step(): pl.pallas_call(functools.partial(step_kernel, n, tp), out_shape=tuple((VM...  64.3 us
    pallas_call x1, Pallas kernels, step(): pl.pallas_call(store_kernel, out_shape=tuple((jax.ShapeDtypeStruct(*resul...  2.21 us

profile of v3, /device:TPU:0, one launch (start us, length us, event | category | flops | bytes accessed | tf_op | source)
XLA Modules:
  0.0 68.4 jit_solution(12032410871021187733)
XLA Ops:
  1.9 64.3 %shard_map.102 = (bf16[128,7168]{1,0:T(8,128)(2,1)S(1)}, f32[64,2048]{1,0:T(8,128)S(1)}, f32[64,7168]{1,0:T(8,128)S(1)}, bf16[64,4096]{1,0:T(8,128)(2,1)S(1)}) custom-call(bf16[64,2048]{1,0:T(8,128)(2,1)} %bitcast.5, bf16[64,7168]{1,0:T(8,128)(2,1)} %bitcast.4, bf16[64,4096]{1,0:T(8,128)(2,1)} %x_ref.1, bf16[128,7168]{1,0:T(8,128)(2,1)} %g_ref.1, ...), custom_call_target="tpu_custom_call" | custom-call | tf_op jit(solution)/shard_map/pallas_call | solution.py:568
  66.2 2.2 %shard_map.103 = (bf16[128,7168]{1,0:T(8,128)(2,1)}, f32[64,2048]{1,0:T(8,128)}, f32[64,7168]{1,0:T(8,128)}, bf16[64,4096]{1,0:T(8,128)(2,1)}) custom-call(bf16[128,7168]{1,0:T(8,128)(2,1)S(1)} %get-tuple-element.12.refs_0_, f32[64,2048]{1,0:T(8,128)S(1)} %get-tuple-element.13.refs_1_, f32[64,7168]{1,0:T(8,128)S(1)} %get-tuple-element.14.refs_2_, ...), custom_call_target="tpu_custom_call" | custom-call | tf_op jit(solution)/shard_map/pallas_call | solution.py:589

commit v4 on v2

--- a/solution.py
+++ b/solution.py
@@ -13,26 +13,31 @@
 VMEM = pltpu.VMEM
 SMEM = pltpu.SMEM
 
-DOWN_FACTOR, UP_FACTOR = "XX", "xxxxxxX"
+DOWN_FACTOR, UP_FACTOR = "XX", "xxzXxxx"
 UP_GRADIENT, DOWN_GRADIENT = "xxxxxxX", "XZ"
-RELAY, LAND, NEAR, SHARE, LEAD, SPREAD, CROSS = 2, 2, 1, 1, 1, 2, 1
-AHEAD, LAG = 4, 6
-
-
-def pieces(width, most):
-    tiles = width // 128
-    count = max(k for k in range(1, most + 1) if tiles % k == 0)
-    step = width // count
-    return [(i * step, step) for i in range(count)]
+DOWN_SHARES, UP_SHARES = (4, 4), (5, 4, 2, 4, 5, 5, 3)
+RELAY, LAND, NEAR, SHARE, LEAD, SPREAD, CROSS = 2, 2, 1, 1, 1, 2, 2
+AHEAD, LAG, PACE = 5, 45, 5
+STORES = 1
+
+
+def pieces(width, shares):
+    tiles, total, seen, start, out = width // 128, sum(shares), 0, 0, []
+    for i, share in enumerate(shares):
+        seen += share
+        end = (2 * seen * tiles + total) // (2 * total)
+        if end > start:
+            out.append((i, start * 128, (end - start) * 128))
+        start = end
+    return out
 
 
 def layout(width, hidden):
-    out = []
-    for which, size, most in (("a", width // 2, len(DOWN_FACTOR)), ("b", hidden // 2, len(UP_FACTOR))):
-        base = 0 if which == "a" else width // 2
-        for i, (start, step) in enumerate(pieces(size, most)):
-            out.append((which, i, start, step, base + start))
-    return out
+    halves = ("a", 0, width // 2, DOWN_SHARES), ("b", width // 2, hidden // 2, UP_SHARES)
+    return [
+        (which, i, start, size, base + start)
+        for which, base, half, shares in halves for i, start, size in pieces(half, shares)
+    ]
 
 
 def greet(n, tp, me, mine, partners):
@@ -525,18 +530,18 @@
 
     for i, j in enumerate(ups):
         plan(max(ready + SHARE, settled_at(j)) + 2, 11, functools.partial(output, j))
-        chain(j, ready + SHARE + i, "down", lambda cols: g[:, cols], adapter_scale)
+        chain(j, ready + SHARE + i * PACE // 4, "down", lambda cols: g[:, cols], adapter_scale)
     whole = max(settled_at(j) for j in ups)
     plan(whole, 2, start_back)
     plan(whole + SHARE, 1, finish_back)
     for i, j in enumerate(downs):
         chain(j, whole + SHARE, "back_low", lambda cols: xt[:, :, cols].reshape(tokens, cols.size), None)
     plan(whole + SHARE, 12, input_gradient)
-    for when_at, _, _, body in sorted(events, key=lambda event: event[:3]):
-        if when_at != tick[0]:
-            tick[0] = when_at
-            drain(when_at - LAG)
-        body()
+    events.sort(key=lambda event: event[:3])
+    for i, event in enumerate(events):
+        tick[0] = i
+        drain(i - LAG)
+        event[3]()
     for j in ups + downs:
         out_copies[j].wait_recv()
     for copy in gx_copies:
@@ -580,7 +585,30 @@
             collective_id=0, has_side_effects=True, vmem_limit_bytes=56 * 1024 * 1024
         ),
     )(a.reshape(own, width), b.reshape(own, hidden), x, g, adapter, live, home)
-    return held
+    anywhere = pl.BlockSpec(memory_space=pl.ANY)
+    return pl.pallas_call(
+        store_kernel,
+        out_shape=tuple(jax.ShapeDtypeStruct(*result) for result in results),
+        in_specs=[inside] * len(results),
+        out_specs=(anywhere,) * len(results),
+        scratch_shapes=[dma((len(results), STORES))],
+        compiler_params=pltpu.CompilerParams(vmem_limit_bytes=1024 * 1024),
+    )(*[pltpu.with_memory_space_constraint(value, VMEM) for value in held])
+
+
+def store_kernel(*refs):
+    sems = refs[-1]
+    number = len(refs) // 2
+    copies = []
+    for i in range(number):
+        rows = refs[i].shape[0] // STORES
+        for k in range(STORES):
+            part = pl.ds(k * rows, rows)
+            copies.append(pltpu.make_async_copy(refs[i].at[part], refs[number + i].at[part], sems.at[i, k]))
+    for copy in copies:
+        copy.start()
+    for copy in copies:
+        copy.wait()
 
 
 def per_device(

time: 70.4 us -> 66.9 us (0.950)
  local copies, waits for them, and re-layouts: 4.04 us -> 0 us
    unnamed x4 -> x0, local copies, waits for them, and re-layouts: 4.04 us -> none
    pallas_call x0 -> x1, Pallas kernels: none -> 2.21 us  [step(): pl.pallas_call(store_kernel, out_shape=tuple((jax.ShapeDtypeStruct(*resul...]
    pallas_call x1, Pallas kernels: 64.3 us -> 62.6 us  [step(): pl.pallas_call(functools.partial(step_kernel, n, tp), out_shape=tuple((VM...]
where the time goes in v4:
time: 66.9 us; the launch traced here: 66.8 us
  Pallas kernels  64.8 us (97%)
  between operations  1.93 us (3%)
    pallas_call x1, Pallas kernels, step(): pl.pallas_call(functools.partial(step_kernel, n, tp), out_shape=tuple((VM...  62.6 us
    pallas_call x1, Pallas kernels, step(): pl.pallas_call(store_kernel, out_shape=tuple((jax.ShapeDtypeStruct(*resul...  2.21 us

profile of v4, /device:TPU:0, one launch (start us, length us, event | category | flops | bytes accessed | tf_op | source)
XLA Modules:
  0.0 66.8 jit_solution(6350146081369936341)
XLA Ops:
  1.9 62.6 %shard_map.102 = (bf16[128,7168]{1,0:T(8,128)(2,1)S(1)}, f32[64,2048]{1,0:T(8,128)S(1)}, f32[64,7168]{1,0:T(8,128)S(1)}, bf16[64,4096]{1,0:T(8,128)(2,1)S(1)}) custom-call(bf16[64,2048]{1,0:T(8,128)(2,1)} %bitcast.5, bf16[64,7168]{1,0:T(8,128)(2,1)} %bitcast.4, bf16[64,4096]{1,0:T(8,128)(2,1)} %x_ref.1, bf16[128,7168]{1,0:T(8,128)(2,1)} %g_ref.1, ...), custom_call_target="tpu_custom_call" | custom-call | tf_op jit(solution)/shard_map/pallas_call | solution.py:568
  64.5 2.2 %shard_map.103 = (bf16[128,7168]{1,0:T(8,128)(2,1)}, f32[64,2048]{1,0:T(8,128)}, f32[64,7168]{1,0:T(8,128)}, bf16[64,4096]{1,0:T(8,128)(2,1)}) custom-call(bf16[128,7168]{1,0:T(8,128)(2,1)S(1)} %get-tuple-element.12.refs_0_, f32[64,2048]{1,0:T(8,128)S(1)} %get-tuple-element.13.refs_1_, f32[64,7168]{1,0:T(8,128)S(1)} %get-tuple-element.14.refs_2_, ...), custom_call_target="tpu_custom_call" | custom-call | tf_op jit(solution)/shard_map/pallas_call | solution.py:589

commit v5 on v4

--- a/solution.py
+++ b/solution.py
@@ -17,7 +17,7 @@
 UP_GRADIENT, DOWN_GRADIENT = "xxxxxxX", "XZ"
 DOWN_SHARES, UP_SHARES = (4, 4), (5, 4, 2, 4, 5, 5, 3)
 RELAY, LAND, NEAR, SHARE, LEAD, SPREAD, CROSS = 2, 2, 1, 1, 1, 2, 2
-AHEAD, LAG, PACE = 5, 45, 5
+AHEAD, LAG, PACE = 6, 45, 5
 STORES = 1
 
 

time: 66.9 us -> 66.9 us (level)
  no operation moved by 1% of the time
where the time goes in v5:
time: 66.9 us; the launch traced here: 66.8 us
  Pallas kernels  64.8 us (97%)
  between operations  1.93 us (3%)
    pallas_call x1, Pallas kernels, step(): pl.pallas_call(functools.partial(step_kernel, n, tp), out_shape=tuple((VM...  62.6 us
    pallas_call x1, Pallas kernels, step(): pl.pallas_call(store_kernel, out_shape=tuple((jax.ShapeDtypeStruct(*resul...  2.21 us

profile of v5, /device:TPU:0, one launch (start us, length us, event | category | flops | bytes accessed | tf_op | source)
XLA Modules:
  0.0 66.8 jit_solution(667831443471034161)
XLA Ops:
  1.9 62.6 %shard_map.102 = (bf16[128,7168]{1,0:T(8,128)(2,1)S(1)}, f32[64,2048]{1,0:T(8,128)S(1)}, f32[64,7168]{1,0:T(8,128)S(1)}, bf16[64,4096]{1,0:T(8,128)(2,1)S(1)}) custom-call(bf16[64,2048]{1,0:T(8,128)(2,1)} %bitcast.5, bf16[64,7168]{1,0:T(8,128)(2,1)} %bitcast.4, bf16[64,4096]{1,0:T(8,128)(2,1)} %x_ref.1, bf16[128,7168]{1,0:T(8,128)(2,1)} %g_ref.1, ...), custom_call_target="tpu_custom_call" | custom-call | tf_op jit(solution)/shard_map/pallas_call | solution.py:568
  64.5 2.2 %shard_map.103 = (bf16[128,7168]{1,0:T(8,128)(2,1)}, f32[64,2048]{1,0:T(8,128)}, f32[64,7168]{1,0:T(8,128)}, bf16[64,4096]{1,0:T(8,128)(2,1)}) custom-call(bf16[128,7168]{1,0:T(8,128)(2,1)S(1)} %get-tuple-element.12.refs_0_, f32[64,2048]{1,0:T(8,128)S(1)} %get-tuple-element.13.refs_1_, f32[64,7168]{1,0:T(8,128)S(1)} %get-tuple-element.14.refs_2_, ...), custom_call_target="tpu_custom_call" | custom-call | tf_op jit(solution)/shard_map/pallas_call | solution.py:589
